TPU v7x, 128 devices: a whole 4x4x4 slice. The times are simulated.
128 devices in a mesh: segment: 4 (over x), col: 32 (over z, y, core).
Axes of the slice: x: 4, y: 4, z: 4, core: 2. Of those that a mesh axis runs over, the one named last changes fastest.
Arguments:
- left_env: bfloat16 [384, 8192], P(None, 'col'), may hold values from -6 to 6
- bit_strings: int32 [384, 4], P(None, 'segment'), may hold values from 0 to 1
- site_tensors: bfloat16 [4, 2, 8192, 8192], P('segment', None, None, 'col'), may hold values from -0.0625 to 0.0625
Outputs:
- section_env: bfloat16 [4, 384, 8192], P('segment', None, 'col')
- section_log: float32 [4, 384], P('segment')
All inputs are finite; a program needn't handle non-finite values. Where the computation divides by a largest or mean magnitude, that divisor is 1e-20 or more.
Results may differ from a plain program's by a relative error of at most 0.0065.
Values may be sent and summed in bfloat16 or wider, within the bound.
No kernel may reach another device: no remote copies, remote signals or barrier semaphores. Data moves between devices by JAX's collectives and lax.ppermute only.
A program may use at most 128 MiB of HBM per device.

v0:
```python
import jax
import jax.numpy as jnp
from jax import lax
from jax.sharding import PartitionSpec as P

MICRO = 2
epsilon = 1e-06


def sent_to_all(value, axis):
    length = lax.axis_size(axis)
    return lax.all_to_all(
        jnp.broadcast_to(value[None], (length, *value.shape)), axis, 0, 0, tiled=True
    )


def taken_together(value, axis):
    everything = sent_to_all(value, axis)
    return jnp.max(everything, axis=0)


def passed_along(value, axis, by):
    length = lax.axis_size(axis)
    pairs = [(i, i + by) for i in range(length) if 0 <= i + by < length]
    return lax.ppermute(value, axis, pairs)


def advance(vector, bit_column, tensor):
    batch_rows = vector.shape[0]
    col_width = tensor.shape[2]
    block = min(128, batch_rows)
    buffer_rows = (batch_rows + block - 1 + block - 1) // block * block
    block_count = buffer_rows // block
    ones_before = jnp.cumsum(bit_column) - bit_column
    index_rows = jnp.arange(batch_rows, dtype=jnp.int32)
    zeros_before = index_rows - ones_before
    zero_count = batch_rows - jnp.sum(bit_column)
    start_one = (zero_count + block - 1) // block * block
    slot = jnp.where(bit_column == 1, start_one + ones_before, zeros_before)
    source = jnp.zeros((buffer_rows,), jnp.int32).at[slot].set(index_rows)
    filled = jnp.zeros((buffer_rows,), jnp.bool_).at[slot].set(True)
    block_bit = (jnp.arange(block_count, dtype=jnp.int32) * block >= start_one).astype(jnp.int32)
    arranged_in = jnp.where(
        filled[:, None], jnp.take(vector, source, axis=0), jnp.zeros((), vector.dtype)
    )
    gathered_piece = lax.all_gather(arranged_in, "col", axis=1, tiled=True)
    width = gathered_piece.shape[1]
    pieces = gathered_piece.reshape(block_count, block, width)

    def one_block(inputs):
        rows_block, bit_value = inputs
        weight_block = lax.dynamic_slice(
            tensor, (bit_value, 0, jnp.int32(0)), (1, width, col_width)
        )[0]
        return jnp.dot(rows_block, weight_block, preferred_element_type=jnp.float32)

    result = lax.map(one_block, (pieces, block_bit))
    arranged_out = result.reshape(buffer_rows, col_width)
    chosen = jnp.take(arranged_out, slot, axis=0)
    maximum = taken_together(jnp.max(jnp.abs(chosen), axis=1), "col") + epsilon
    return ((chosen / maximum[:, None]).astype(jnp.bfloat16), jnp.log(maximum))


def local(left_env, bit_strings, site_tensors):
    segment_count = lax.axis_size("segment")
    segment_index = lax.axis_index("segment")
    row_count = left_env.shape[0]
    col_width = left_env.shape[1]
    granules = MICRO
    batch_rows = row_count // granules
    env_out = jnp.zeros((row_count, col_width), jnp.bfloat16)
    log_out = jnp.zeros((row_count,), jnp.float32)
    incoming = jnp.zeros((batch_rows, col_width), jnp.bfloat16)
    tick_total = granules + segment_count - 1
    for tick_step in range(tick_total):
        position = tick_step - segment_index
        active = (position >= 0) & (position < granules)
        offset_rows = jnp.clip(position, 0, granules - 1) * batch_rows
        from_input = lax.dynamic_slice_in_dim(left_env, offset_rows, batch_rows, 0)
        current = jnp.where(segment_index == 0, from_input, incoming)
        bit_block = lax.dynamic_slice_in_dim(bit_strings, offset_rows, batch_rows, 0)
        current, logs_site = advance(current, bit_block[:, 0], site_tensors[0])
        old_env = lax.dynamic_slice_in_dim(env_out, offset_rows, batch_rows, 0)
        old_log = lax.dynamic_slice_in_dim(log_out, offset_rows, batch_rows, 0)
        env_out = lax.dynamic_update_slice_in_dim(
            env_out, jnp.where(active, current, old_env), offset_rows, 0
        )
        log_out = lax.dynamic_update_slice_in_dim(
            log_out, jnp.where(active, logs_site, old_log), offset_rows, 0
        )
        if tick_step + 1 < tick_total:
            incoming = passed_along(current, "segment", 1)
    return (env_out[None], log_out[None])


def solution(mesh):
    placed = (P(None, "col"), P(None, "segment"), P("segment", None, None, "col"))
    return jax.shard_map(
        local,
        mesh=mesh,
        in_specs=placed,
        out_specs=(P("segment", None, "col"), P("segment", None)),
        check_vma=False,
    )
```

profile of v0, /device:TPU:1, one launch (start us, length us, event | category | flops | bytes accessed | tf_op | source)
XLA Modules:
  0.0 496.4 jit_solution(4290405413867485066)
XLA Ops:
  20.4 54.5 %all-gather.6.cloned.1.call-done = bf16[384,8192]{1,0:T(8,128)(2,1)} async-done(((bf16[384,256]{1,0:T(8,128)(2,1)}), bf16[384,8192]{1,0:T(8,128)(2,1)}) %all-gather.6.cloned.1.call-update) | async-done | bytes 6291472 | tf_op jit(solution)/shard_map/all_gather | solution.py:46
  75.0 18.3 %while.50 = (s32[]{:T(128)}, f32[3,128,256]{2,1,0:T(8,128)S(1)}, bf16[3,128,8192]{2,1,0:T(8,128)(2,1)}, s32[3]{0:T(128)S(1)}, bf16[2,8192,256]{2,1,0:T(8,128)(2,1)}, /*index=5*/s32[]{:T(128)}, s32[]{:T(128)}, s32[]{:T(128)}) while((s32[]{:T(128)}, f32[3,128,256]{2,1,0:T(8,128)S(1)}, bf16[3,128,8192]{2,1,0:T(8,128)(2,1)}, s32[3]{0:T(128)S(1)}, ...), condition=%wide.region_6.8_spmd, body=%wide.region_5.7_spmd.sunk | while | flops 536870912 | bytes 6423687 | solution.py:57
  83.6 3.5 fusion.123
  89.7 3.5 fusion.123
  95.0 5.5 %all-to-all-start = ((f32[32,1,192]{2,1,0:T(1,128)}), f32[32,1,192]{2,1,0:T(1,128)S(1)}, u32[]{:S(2)}, u32[]{:S(2)}) async-start(f32[32,1,192]{2,1,0:T(1,128)} %broadcast_in_dim.147), calls=%async_computation | async-start | bytes 65536 | tf_op jit(solution)/shard_map/all_to_all | solution.py:12
  101.8 5.9 %all-to-all-done = f32[32,1,192]{2,1,0:T(1,128)S(1)} async-done(((f32[32,1,192]{2,1,0:T(1,128)}), f32[32,1,192]{2,1,0:T(1,128)S(1)}, u32[]{:S(2)}, u32[]{:S(2)}) %all-to-all-start) | async-done | bytes 24608 | tf_op jit(solution)/shard_map/all_to_all | solution.py:12
  117.0 53.0 %all-gather.8.cloned.1.call-done = bf16[384,8192]{1,0:T(8,128)(2,1)} async-done(((bf16[384,256]{1,0:T(8,128)(2,1)}), bf16[384,8192]{1,0:T(8,128)(2,1)}) %all-gather.8.cloned.1.call-update) | async-done | bytes 6291472 | tf_op jit(solution)/shard_map/all_gather | solution.py:46
  170.1 18.3 %while.51 = (s32[]{:T(128)}, f32[3,128,256]{2,1,0:T(8,128)S(1)}, bf16[3,128,8192]{2,1,0:T(8,128)(2,1)}, s32[3]{0:T(128)S(1)}, bf16[2,8192,256]{2,1,0:T(8,128)(2,1)}, /*index=5*/s32[]{:T(128)}, s32[]{:T(128)}, s32[]{:T(128)}) while((s32[]{:T(128)}, f32[3,128,256]{2,1,0:T(8,128)S(1)}, bf16[3,128,8192]{2,1,0:T(8,128)(2,1)}, s32[3]{0:T(128)S(1)}, ...), condition=%wide.region_15.18_spmd, body=%wide.region_14.17_spmd.sunk | while | flops 536870912 | bytes 6423687 | solution.py:57
  172.6 3.5 fusion.126
  178.7 3.5 fusion.126
  184.8 3.5 fusion.126
  190.1 5.5 %all-to-all-start.1 = ((f32[32,1,192]{2,1,0:T(1,128)}), f32[32,1,192]{2,1,0:T(1,128)S(1)}, u32[]{:S(2)}, u32[]{:S(2)}) async-start(f32[32,1,192]{2,1,0:T(1,128)} %broadcast_in_dim.150), calls=%async_computation.1 | async-start | bytes 65536 | tf_op jit(solution)/shard_map/all_to_all | solution.py:12
  196.9 5.9 %all-to-all-done.1 = f32[32,1,192]{2,1,0:T(1,128)S(1)} async-done(((f32[32,1,192]{2,1,0:T(1,128)}), f32[32,1,192]{2,1,0:T(1,128)S(1)}, u32[]{:S(2)}, u32[]{:S(2)}) %all-to-all-start.1) | async-done | bytes 24608 | tf_op jit(solution)/shard_map/all_to_all | solution.py:12
  214.7 50.5 %all-gather.10.cloned.1.call-done = bf16[384,8192]{1,0:T(8,128)(2,1)} async-done(((bf16[384,256]{1,0:T(8,128)(2,1)}), bf16[384,8192]{1,0:T(8,128)(2,1)}) %all-gather.10.cloned.1.call-update) | async-done | bytes 6291472 | tf_op jit(solution)/shard_map/all_gather | solution.py:46
  265.2 18.3 %while.52 = (s32[]{:T(128)}, f32[3,128,256]{2,1,0:T(8,128)S(1)}, bf16[3,128,8192]{2,1,0:T(8,128)(2,1)}, s32[3]{0:T(128)S(1)}, bf16[2,8192,256]{2,1,0:T(8,128)(2,1)}, /*index=5*/s32[]{:T(128)}, s32[]{:T(128)}, s32[]{:T(128)}) while((s32[]{:T(128)}, f32[3,128,256]{2,1,0:T(8,128)S(1)}, bf16[3,128,8192]{2,1,0:T(8,128)(2,1)}, s32[3]{0:T(128)S(1)}, ...), condition=%wide.region_24.27_spmd, body=%wide.region_23.26_spmd.sunk | while | flops 536870912 | bytes 6423687 | solution.py:57
  267.8 3.5 fusion.129
  273.9 3.5 fusion.129
  280.0 3.5 fusion.129
  285.2 5.5 %all-to-all-start.2 = ((f32[32,1,192]{2,1,0:T(1,128)}), f32[32,1,192]{2,1,0:T(1,128)S(1)}, u32[]{:S(2)}, u32[]{:S(2)}) async-start(f32[32,1,192]{2,1,0:T(1,128)} %broadcast_in_dim.153), calls=%async_computation.2 | async-start | bytes 65536 | tf_op jit(solution)/shard_map/all_to_all | solution.py:12
  292.1 5.9 %all-to-all-done.2 = f32[32,1,192]{2,1,0:T(1,128)S(1)} async-done(((f32[32,1,192]{2,1,0:T(1,128)}), f32[32,1,192]{2,1,0:T(1,128)S(1)}, u32[]{:S(2)}, u32[]{:S(2)}) %all-to-all-start.2) | async-done | bytes 24608 | tf_op jit(solution)/shard_map/all_to_all | solution.py:12
  307.3 53.0 %all-gather.12.cloned.1.call-done = bf16[384,8192]{1,0:T(8,128)(2,1)} async-done(((bf16[384,256]{1,0:T(8,128)(2,1)}), bf16[384,8192]{1,0:T(8,128)(2,1)}) %all-gather.12.cloned.1.call-update) | async-done | bytes 6291472 | tf_op jit(solution)/shard_map/all_gather | solution.py:46
  360.4 18.3 %while.53 = (s32[]{:T(128)}, f32[3,128,256]{2,1,0:T(8,128)S(1)}, bf16[3,128,8192]{2,1,0:T(8,128)(2,1)}, s32[3]{0:T(128)S(1)}, bf16[2,8192,256]{2,1,0:T(8,128)(2,1)}, /*index=5*/s32[]{:T(128)}, s32[]{:T(128)}, s32[]{:T(128)}) while((s32[]{:T(128)}, f32[3,128,256]{2,1,0:T(8,128)S(1)}, bf16[3,128,8192]{2,1,0:T(8,128)(2,1)}, s32[3]{0:T(128)S(1)}, ...), condition=%wide.region_33.36_spmd, body=%wide.region_32.35_spmd.sunk | while | flops 536870912 | bytes 6423687 | solution.py:57
  362.9 3.5 fusion.132
  375.1 3.5 fusion.132
  380.4 5.5 %all-to-all-start.3 = ((f32[32,1,192]{2,1,0:T(1,128)}), f32[32,1,192]{2,1,0:T(1,128)S(1)}, u32[]{:S(2)}, u32[]{:S(2)}) async-start(f32[32,1,192]{2,1,0:T(1,128)} %broadcast_in_dim.156), calls=%async_computation.3 | async-start | bytes 65536 | tf_op jit(solution)/shard_map/all_to_all | solution.py:12
  387.2 5.9 %all-to-all-done.3 = f32[32,1,192]{2,1,0:T(1,128)S(1)} async-done(((f32[32,1,192]{2,1,0:T(1,128)}), f32[32,1,192]{2,1,0:T(1,128)S(1)}, u32[]{:S(2)}, u32[]{:S(2)}) %all-to-all-start.3) | async-done | bytes 24608 | tf_op jit(solution)/shard_map/all_to_all | solution.py:12
  401.2 54.3 %all-gather.14.cloned.1.call-done = bf16[384,8192]{1,0:T(8,128)(2,1)} async-done(((bf16[384,256]{1,0:T(8,128)(2,1)}), bf16[384,8192]{1,0:T(8,128)(2,1)}) %all-gather.14.cloned.1.call-update) | async-done | bytes 6291472 | tf_op jit(solution)/shard_map/all_gather | solution.py:46
  455.5 18.3 %while.54 = (s32[]{:T(128)}, f32[3,128,256]{2,1,0:T(8,128)S(1)}, bf16[3,128,8192]{2,1,0:T(8,128)(2,1)}, s32[3]{0:T(128)S(1)}, bf16[2,8192,256]{2,1,0:T(8,128)(2,1)}, /*index=5*/s32[]{:T(128)}, s32[]{:T(128)}, s32[]{:T(128)}) while((s32[]{:T(128)}, f32[3,128,256]{2,1,0:T(8,128)S(1)}, bf16[3,128,8192]{2,1,0:T(8,128)(2,1)}, s32[3]{0:T(128)S(1)}, ...), condition=%wide.region_42.45_spmd, body=%wide.region_41.44_spmd.sunk | while | flops 536870912 | bytes 6423687 | solution.py:57
  464.2 3.5 fusion.135
  470.3 3.5 fusion.135
  475.5 5.5 %all-to-all-start.4 = ((f32[32,1,192]{2,1,0:T(1,128)}), f32[32,1,192]{2,1,0:T(1,128)S(1)}, u32[]{:S(2)}, u32[]{:S(2)}) async-start(f32[32,1,192]{2,1,0:T(1,128)} %broadcast_in_dim.160), calls=%async_computation.4 | async-start | bytes 65536 | tf_op jit(solution)/shard_map/all_to_all | solution.py:12
  481.1 7.2 %all-to-all-done.4 = f32[32,1,192]{2,1,0:T(1,128)S(1)} async-done(((f32[32,1,192]{2,1,0:T(1,128)}), f32[32,1,192]{2,1,0:T(1,128)S(1)}, u32[]{:S(2)}, u32[]{:S(2)}) %all-to-all-start.4) | async-done | bytes 24608 | tf_op jit(solution)/shard_map/all_to_all | solution.py:12
  (172 shorter events, 82.8 us)
Async XLA Ops:
  7.2 67.8 %all-gather.6.cloned.1.call-start = ((), (), s32[]{:S(2)}) async-start(), calls=%async_computation.5 | async-start | bytes 6488064 | tf_op jit(solution)/shard_map/all_gather | solution.py:46
  75.0 37.8 %copy-start = (bf16[384,256]{1,0:T(8,128)(2,1)S(1)}, bf16[384,256]{1,0:T(8,128)(2,1)}, u32[]{:S(2)}) copy-start(bf16[384,256]{1,0:T(8,128)(2,1)} %param.17) | copy-start | bytes 589828
  95.0 12.8 %all-to-all-start = ((f32[32,1,192]{2,1,0:T(1,128)}), f32[32,1,192]{2,1,0:T(1,128)S(1)}, u32[]{:S(2)}, u32[]{:S(2)}) async-start(f32[32,1,192]{2,1,0:T(1,128)} %broadcast_in_dim.147), calls=%async_computation | async-start | bytes 65536 | tf_op jit(solution)/shard_map/all_to_all | solution.py:12
  100.5 69.6 %all-gather.8.cloned.1.call-start = ((), (), s32[]{:S(2)}) async-start(), calls=%async_computation.6 | async-start | bytes 6488064 | tf_op jit(solution)/shard_map/all_gather | solution.py:46
  108.1 4.7 collective-permute-start
  190.1 12.8 %all-to-all-start.1 = ((f32[32,1,192]{2,1,0:T(1,128)}), f32[32,1,192]{2,1,0:T(1,128)S(1)}, u32[]{:S(2)}, u32[]{:S(2)}) async-start(f32[32,1,192]{2,1,0:T(1,128)} %broadcast_in_dim.150), calls=%async_computation.1 | async-start | bytes 65536 | tf_op jit(solution)/shard_map/all_to_all | solution.py:12
  195.6 69.6 %all-gather.10.cloned.1.call-start = ((), (), s32[]{:S(2)}) async-start(), calls=%async_computation.7 | async-start | bytes 6488064 | tf_op jit(solution)/shard_map/all_gather | solution.py:46
  203.2 4.7 collective-permute-start.1
  285.2 12.8 %all-to-all-start.2 = ((f32[32,1,192]{2,1,0:T(1,128)}), f32[32,1,192]{2,1,0:T(1,128)S(1)}, u32[]{:S(2)}, u32[]{:S(2)}) async-start(f32[32,1,192]{2,1,0:T(1,128)} %broadcast_in_dim.153), calls=%async_computation.2 | async-start | bytes 65536 | tf_op jit(solution)/shard_map/all_to_all | solution.py:12
  290.8 69.6 %all-gather.12.cloned.1.call-start = ((), (), s32[]{:S(2)}) async-start(), calls=%async_computation.8 | async-start | bytes 6488064 | tf_op jit(solution)/shard_map/all_gather | solution.py:46
  298.4 4.7 collective-permute-start.2
  380.4 12.8 %all-to-all-start.3 = ((f32[32,1,192]{2,1,0:T(1,128)}), f32[32,1,192]{2,1,0:T(1,128)S(1)}, u32[]{:S(2)}, u32[]{:S(2)}) async-start(f32[32,1,192]{2,1,0:T(1,128)} %broadcast_in_dim.156), calls=%async_computation.3 | async-start | bytes 65536 | tf_op jit(solution)/shard_map/all_to_all | solution.py:12
  385.9 69.6 %all-gather.14.cloned.1.call-start = ((), (), s32[]{:S(2)}) async-start(), calls=%async_computation.9 | async-start | bytes 6488064 | tf_op jit(solution)/shard_map/all_gather | solution.py:46
  393.5 4.7 collective-permute-start.3
  475.5 12.8 %all-to-all-start.4 = ((f32[32,1,192]{2,1,0:T(1,128)}), f32[32,1,192]{2,1,0:T(1,128)S(1)}, u32[]{:S(2)}, u32[]{:S(2)}) async-start(f32[32,1,192]{2,1,0:T(1,128)} %broadcast_in_dim.160), calls=%async_computation.4 | async-start | bytes 65536 | tf_op jit(solution)/shard_map/all_to_all | solution.py:12
  488.6 0.6 copy-start.2
  489.2 0.7 copy-start.1
Sparse Core Ops, SparseCore 0:
  16.7 58.1 all-gather.5
  115.9 54.1 all-gather.7
  211.0 54.1 all-gather.9
  306.2 54.1 all-gather.11
  401.3 54.1 all-gather.13
where the time goes:
time: 497 us; the launch traced here: 496 us
  waiting for transfers between devices  303 us (61%)
  matrix products  53.1 us (11%)
  local copies, waits for them, and re-layouts  41.3 us (8%)
  starting transfers between devices  40.3 us (8%)
  loops' own time  29.5 us (6%)
  between operations  17.7 us (4%)
  other arithmetic  11.8 us (2%)
    all_gather x5, waiting for transfers between devices, advance(): gathered_piece = lax.all_gather(arranged_in, 'col', axis=1, tiled=True)  265 us
    dot_general x15, matrix products, one_block(): return jnp.dot(rows_block, weight_block, preferred_element_type=jnp.float32)  53.1 us
    all_to_all x5, waiting for transfers between devices, sent_to_all(): lax.all_to_all(jnp.broadcast_to(value[None], (length, *value.shape)), axi...  30.9 us
    another operation x5, loops' own time, advance(): result = lax.map(one_block, (pieces, block_bit))  29.5 us
    all_to_all x5, starting transfers between devices, sent_to_all(): lax.all_to_all(jnp.broadcast_to(value[None], (length, *value.shape)), axi...  27.5 us
    ppermute x4, starting transfers between devices, passed_along(): return lax.ppermute(value, axis, pairs)  12.6 us
    gather x5, local copies, waits for them, and re-layouts, advance(): jnp.take(vector, source, axis=0)  10.3 us
  transfers between devices with their start and end apart: 14, of which 14 were waited for; matrix products, arithmetic and copies ran while one was open for 3% of the time, Pallas kernels for 0%

commit v1 on v0

--- a/solution.py
+++ b/solution.py
@@ -43,7 +43,9 @@
     arranged_in = jnp.where(
         filled[:, None], jnp.take(vector, source, axis=0), jnp.zeros((), vector.dtype)
     )
-    gathered_piece = lax.all_gather(arranged_in, "col", axis=1, tiled=True)
+    gathered_piece = jnp.concatenate(
+        lax.all_to_all(jnp.stack([arranged_in] * lax.axis_size("col")), "col", 0, 0), axis=1
+    )
     width = gathered_piece.shape[1]
     pieces = gathered_piece.reshape(block_count, block, width)
 

time: 497 us -> 748 us (1.51); the launches traced: 496 us -> 737 us
  local copies, waits for them, and re-layouts: 41.3 us -> 156 us
  waiting for transfers between devices: 303 us -> 392 us
  starting transfers between devices: 40.3 us -> 93 us
  between operations: 17.7 us -> 4.94 us
    all_to_all x0 -> x5, waiting for transfers between devices: none -> 354 us  [advance(): lax.all_to_all(jnp.stack([arranged_in] * lax.axis_size('col')), 'col', 0, 0)]
    all_gather x5 -> x0, waiting for transfers between devices: 265 us -> none  [advance(): gathered_piece = lax.all_gather(arranged_in, 'col', axis=1, tiled=True)]
    another operation x19 -> x29, local copies, waits for them, and re-layouts: 1.02 us -> 70 us  [the longest x5 52.2 us: advance(): pieces = gathered_piece.reshape(block_count, block, width)]
    reshape x1 -> x6, local copies, waits for them, and re-layouts: 0.01 us -> 45 us  [the longest x5 45 us: advance(): jnp.concatenate(lax.all_to_all(jnp.stack([arranged_in] * lax.axis_size('c...]
    all_to_all x0 -> x5, starting transfers between devices: none -> 33.8 us  [advance(): lax.all_to_all(jnp.stack([arranged_in] * lax.axis_size('col')), 'col', 0, 0)]
    all_to_all x5, starting transfers between devices: 27.5 us -> 43.6 us  [sent_to_all(): lax.all_to_all(jnp.broadcast_to(value[None], (length, *value.shape)), axi...]
  transfers between devices with their start and end apart: 14 -> 14, of which waited for: 14 -> 14; matrix products, arithmetic and copies ran while one was open for 3% -> 2% of each run, Pallas kernels for 0% -> 0%
where the time goes in v1:
time: 748 us; the launch traced here: 737 us
  waiting for transfers between devices  392 us (52%)
  local copies, waits for them, and re-layouts  156 us (21%)
  starting transfers between devices  93 us (12%)
  matrix products  53.1 us (7%)
  loops' own time  29.5 us (4%)
  other arithmetic  8.44 us (1%)
    all_to_all x5, waiting for transfers between devices, advance(): lax.all_to_all(jnp.stack([arranged_in] * lax.axis_size('col')), 'col', 0, 0)  354 us
    dot_general x15, matrix products, one_block(): return jnp.dot(rows_block, weight_block, preferred_element_type=jnp.float32)  53.1 us
    another operation x5, local copies, waits for them, and re-layouts, advance(): pieces = gathered_piece.reshape(block_count, block, width)  52.2 us
    reshape x5, local copies, waits for them, and re-layouts, advance(): jnp.concatenate(lax.all_to_all(jnp.stack([arranged_in] * lax.axis_size('c...  45 us
    all_to_all x5, starting transfers between devices, sent_to_all(): lax.all_to_all(jnp.broadcast_to(value[None], (length, *value.shape)), axi...  43.6 us
    all_to_all x5, starting transfers between devices, advance(): lax.all_to_all(jnp.stack([arranged_in] * lax.axis_size('col')), 'col', 0, 0)  33.8 us
    all_to_all x5, waiting for transfers between devices, sent_to_all(): lax.all_to_all(jnp.broadcast_to(value[None], (length, *value.shape)), axi...  31.6 us
    another operation x5, loops' own time, advance(): result = lax.map(one_block, (pieces, block_bit))  29.5 us
  transfers between devices with their start and end apart: 14, of which 14 were waited for; matrix products, arithmetic and copies ran while one was open for 2% of the time, Pallas kernels for 0%

profile of v1, /device:TPU:1, one launch (start us, length us, event | category | flops | bytes accessed | tf_op | source)
XLA Modules:
  0.0 736.9 jit_solution(12527223140972619601)
XLA Ops:
  12.8 9.7 %all-to-all-start = ((bf16[32,384,256]{2,1,0:T(8,128)(2,1)}), bf16[32,384,256]{2,1,0:T(8,128)(2,1)}, u32[]{:S(2)}, u32[]{:S(2)}) async-start(bf16[32,384,256]{2,1,0:T(8,128)(2,1)} %stack.10), calls=%async_computation | async-start | bytes 12582912 | tf_op jit(solution)/shard_map/all_to_all | solution.py:47
  26.2 69.1 %all-to-all-done = bf16[32,384,256]{2,1,0:T(8,128)(2,1)} async-done(((bf16[32,384,256]{2,1,0:T(8,128)(2,1)}), bf16[32,384,256]{2,1,0:T(8,128)(2,1)}, u32[]{:S(2)}, u32[]{:S(2)}) %all-to-all-start) | async-done | bytes 6291488 | tf_op jit(solution)/shard_map/all_to_all | solution.py:47
  95.4 9.0 %copy.15 = bf16[384,32,256]{2,1,0:T(8,128)(2,1)} copy(bf16[384,32,256]{2,0,1:T(8,128)(2,1)} %bitcast.23) | data formatting | bytes 12582912 | tf_op jit(solution)/shard_map/reshape | solution.py:46
  104.4 10.4 %reshape_reshape.15 = bf16[3,128,8192]{2,1,0:T(8,128)(2,1)} reshape(bf16[384,32,256]{2,1,0:T(8,128)(2,1)} %copy.15) | data formatting | bytes 12582912 | tf_op jit(solution)/shard_map/reshape;reshape | solution.py:50
  114.8 18.3 %while.50 = (s32[]{:T(128)}, f32[3,128,256]{2,1,0:T(8,128)S(1)}, bf16[3,128,8192]{2,1,0:T(8,128)(2,1)}, s32[3]{0:T(128)S(1)}, bf16[2,8192,256]{2,1,0:T(8,128)(2,1)}, /*index=5*/s32[]{:T(128)}, s32[]{:T(128)}, s32[]{:T(128)}) while((s32[]{:T(128)}, f32[3,128,256]{2,1,0:T(8,128)S(1)}, bf16[3,128,8192]{2,1,0:T(8,128)(2,1)}, s32[3]{0:T(128)S(1)}, ...), condition=%wide.region_6.8_spmd, body=%wide.region_5.7_spmd.sunk | while | flops 536870912 | bytes 6423687 | solution.py:59
  134.9 8.7 %all-to-all-start.1 = ((f32[32,1,192]{2,1,0:T(1,128)}), f32[32,1,192]{2,1,0:T(1,128)S(1)}, u32[]{:S(2)}, u32[]{:S(2)}) async-start(f32[32,1,192]{2,1,0:T(1,128)} %broadcast_in_dim.147), calls=%async_computation.1 | async-start | bytes 65536 | tf_op jit(solution)/shard_map/all_to_all | solution.py:12
  144.9 6.1 all-to-all-done.1
  168.8 71.8 %all-to-all-done.2 = bf16[32,384,256]{2,1,0:T(8,128)(2,1)} async-done(((bf16[32,384,256]{2,1,0:T(8,128)(2,1)}), bf16[32,384,256]{2,1,0:T(8,128)(2,1)}, u32[]{:S(2)}, u32[]{:S(2)}) %all-to-all-start.2) | async-done | bytes 6291488 | tf_op jit(solution)/shard_map/all_to_all | solution.py:47
  240.6 9.0 %copy.17 = bf16[384,32,256]{2,1,0:T(8,128)(2,1)} copy(bf16[384,32,256]{2,0,1:T(8,128)(2,1)} %bitcast.29) | data formatting | bytes 12582912 | tf_op jit(solution)/shard_map/reshape | solution.py:46
  249.6 10.4 %reshape_reshape.16 = bf16[3,128,8192]{2,1,0:T(8,128)(2,1)} reshape(bf16[384,32,256]{2,1,0:T(8,128)(2,1)} %copy.17) | data formatting | bytes 12582912 | tf_op jit(solution)/shard_map/reshape;reshape | solution.py:50
  260.0 18.3 %while.51 = (s32[]{:T(128)}, f32[3,128,256]{2,1,0:T(8,128)S(1)}, bf16[3,128,8192]{2,1,0:T(8,128)(2,1)}, s32[3]{0:T(128)S(1)}, bf16[2,8192,256]{2,1,0:T(8,128)(2,1)}, /*index=5*/s32[]{:T(128)}, s32[]{:T(128)}, s32[]{:T(128)}) while((s32[]{:T(128)}, f32[3,128,256]{2,1,0:T(8,128)S(1)}, bf16[3,128,8192]{2,1,0:T(8,128)(2,1)}, s32[3]{0:T(128)S(1)}, ...), condition=%wide.region_15.18_spmd, body=%wide.region_14.17_spmd.sunk | while | flops 536870912 | bytes 6423687 | solution.py:59
  280.0 8.8 %all-to-all-start.3 = ((f32[32,1,192]{2,1,0:T(1,128)}), f32[32,1,192]{2,1,0:T(1,128)S(1)}, u32[]{:S(2)}, u32[]{:S(2)}) async-start(f32[32,1,192]{2,1,0:T(1,128)} %broadcast_in_dim.150), calls=%async_computation.3 | async-start | bytes 65536 | tf_op jit(solution)/shard_map/all_to_all | solution.py:12
  290.1 6.1 all-to-all-done.3
  307.9 6.2 all-to-all-start.4
  318.0 69.0 %all-to-all-done.4 = bf16[32,384,256]{2,1,0:T(8,128)(2,1)} async-done(((bf16[32,384,256]{2,1,0:T(8,128)(2,1)}), bf16[32,384,256]{2,1,0:T(8,128)(2,1)}, u32[]{:S(2)}, u32[]{:S(2)}) %all-to-all-start.4) | async-done | bytes 6291488 | tf_op jit(solution)/shard_map/all_to_all | solution.py:47
  387.0 9.0 %copy.19 = bf16[384,32,256]{2,1,0:T(8,128)(2,1)} copy(bf16[384,32,256]{2,0,1:T(8,128)(2,1)} %bitcast.34) | data formatting | bytes 12582912 | tf_op jit(solution)/shard_map/reshape | solution.py:46
  396.1 10.4 %reshape_reshape.17 = bf16[3,128,8192]{2,1,0:T(8,128)(2,1)} reshape(bf16[384,32,256]{2,1,0:T(8,128)(2,1)} %copy.19) | data formatting | bytes 12582912 | tf_op jit(solution)/shard_map/reshape;reshape | solution.py:50
  406.5 18.3 %while.52 = (s32[]{:T(128)}, f32[3,128,256]{2,1,0:T(8,128)S(1)}, bf16[3,128,8192]{2,1,0:T(8,128)(2,1)}, s32[3]{0:T(128)S(1)}, bf16[2,8192,256]{2,1,0:T(8,128)(2,1)}, /*index=5*/s32[]{:T(128)}, s32[]{:T(128)}, s32[]{:T(128)}) while((s32[]{:T(128)}, f32[3,128,256]{2,1,0:T(8,128)S(1)}, bf16[3,128,8192]{2,1,0:T(8,128)(2,1)}, s32[3]{0:T(128)S(1)}, ...), condition=%wide.region_24.27_spmd, body=%wide.region_23.26_spmd.sunk | while | flops 536870912 | bytes 6423687 | solution.py:59
  426.5 8.6 %all-to-all-start.5 = ((f32[32,1,192]{2,1,0:T(1,128)}), f32[32,1,192]{2,1,0:T(1,128)S(1)}, u32[]{:S(2)}, u32[]{:S(2)}) async-start(f32[32,1,192]{2,1,0:T(1,128)} %broadcast_in_dim.153), calls=%async_computation.5 | async-start | bytes 65536 | tf_op jit(solution)/shard_map/all_to_all | solution.py:12
  461.8 71.4 %all-to-all-done.6 = bf16[32,384,256]{2,1,0:T(8,128)(2,1)} async-done(((bf16[32,384,256]{2,1,0:T(8,128)(2,1)}), bf16[32,384,256]{2,1,0:T(8,128)(2,1)}, u32[]{:S(2)}, u32[]{:S(2)}) %all-to-all-start.6) | async-done | bytes 6291488 | tf_op jit(solution)/shard_map/all_to_all | solution.py:47
  533.2 9.0 %copy.21 = bf16[384,32,256]{2,1,0:T(8,128)(2,1)} copy(bf16[384,32,256]{2,0,1:T(8,128)(2,1)} %bitcast.39) | data formatting | bytes 12582912 | tf_op jit(solution)/shard_map/reshape | solution.py:46
  542.2 10.4 %reshape_reshape.18 = bf16[3,128,8192]{2,1,0:T(8,128)(2,1)} reshape(bf16[384,32,256]{2,1,0:T(8,128)(2,1)} %copy.21) | data formatting | bytes 12582912 | tf_op jit(solution)/shard_map/reshape;reshape | solution.py:50
  552.6 18.3 %while.53 = (s32[]{:T(128)}, f32[3,128,256]{2,1,0:T(8,128)S(1)}, bf16[3,128,8192]{2,1,0:T(8,128)(2,1)}, s32[3]{0:T(128)S(1)}, bf16[2,8192,256]{2,1,0:T(8,128)(2,1)}, /*index=5*/s32[]{:T(128)}, s32[]{:T(128)}, s32[]{:T(128)}) while((s32[]{:T(128)}, f32[3,128,256]{2,1,0:T(8,128)S(1)}, bf16[3,128,8192]{2,1,0:T(8,128)(2,1)}, s32[3]{0:T(128)S(1)}, ...), condition=%wide.region_33.36_spmd, body=%wide.region_32.35_spmd.sunk | while | flops 536870912 | bytes 6423687 | solution.py:59
  572.6 8.8 %all-to-all-start.7 = ((f32[32,1,192]{2,1,0:T(1,128)}), f32[32,1,192]{2,1,0:T(1,128)S(1)}, u32[]{:S(2)}, u32[]{:S(2)}) async-start(f32[32,1,192]{2,1,0:T(1,128)} %broadcast_in_dim.156), calls=%async_computation.7 | async-start | bytes 65536 | tf_op jit(solution)/shard_map/all_to_all | solution.py:12
  582.7 6.1 all-to-all-done.7
  600.5 6.2 all-to-all-start.8
  606.8 72.8 %all-to-all-done.8 = bf16[32,384,256]{2,1,0:T(8,128)(2,1)} async-done(((bf16[32,384,256]{2,1,0:T(8,128)(2,1)}), bf16[32,384,256]{2,1,0:T(8,128)(2,1)}, u32[]{:S(2)}, u32[]{:S(2)}) %all-to-all-start.8) | async-done | bytes 6291488 | tf_op jit(solution)/shard_map/all_to_all | solution.py:47
  679.6 9.0 %copy.23 = bf16[384,32,256]{2,1,0:T(8,128)(2,1)} copy(bf16[384,32,256]{2,0,1:T(8,128)(2,1)} %bitcast.45) | data formatting | bytes 12582912 | tf_op jit(solution)/shard_map/reshape | solution.py:46
  688.6 10.4 %reshape_reshape.19 = bf16[3,128,8192]{2,1,0:T(8,128)(2,1)} reshape(bf16[384,32,256]{2,1,0:T(8,128)(2,1)} %copy.23) | data formatting | bytes 12582912 | tf_op jit(solution)/shard_map/reshape;reshape | solution.py:50
  699.1 18.3 %while.54 = (s32[]{:T(128)}, f32[3,128,256]{2,1,0:T(8,128)S(1)}, bf16[3,128,8192]{2,1,0:T(8,128)(2,1)}, s32[3]{0:T(128)S(1)}, bf16[2,8192,256]{2,1,0:T(8,128)(2,1)}, /*index=5*/s32[]{:T(128)}, s32[]{:T(128)}, s32[]{:T(128)}) while((s32[]{:T(128)}, f32[3,128,256]{2,1,0:T(8,128)S(1)}, bf16[3,128,8192]{2,1,0:T(8,128)(2,1)}, s32[3]{0:T(128)S(1)}, ...), condition=%wide.region_42.45_spmd, body=%wide.region_41.44_spmd.sunk | while | flops 536870912 | bytes 6423687 | solution.py:59
  719.1 8.6 %all-to-all-start.9 = ((f32[32,1,192]{2,1,0:T(1,128)}), f32[32,1,192]{2,1,0:T(1,128)S(1)}, u32[]{:S(2)}, u32[]{:S(2)}) async-start(f32[32,1,192]{2,1,0:T(1,128)} %broadcast_in_dim.160), calls=%async_computation.9 | async-start | bytes 65536 | tf_op jit(solution)/shard_map/all_to_all | solution.py:12
  727.8 7.3 all-to-all-done.9
  (182 shorter events, 159.8 us)
Async XLA Ops:
  12.8 82.6 %all-to-all-start = ((bf16[32,384,256]{2,1,0:T(8,128)(2,1)}), bf16[32,384,256]{2,1,0:T(8,128)(2,1)}, u32[]{:S(2)}, u32[]{:S(2)}) async-start(bf16[32,384,256]{2,1,0:T(8,128)(2,1)} %stack.10), calls=%async_computation | async-start | bytes 12582912 | tf_op jit(solution)/shard_map/all_to_all | solution.py:47
  114.8 41.2 %copy-start = (bf16[384,256]{1,0:T(8,128)(2,1)S(1)}, bf16[384,256]{1,0:T(8,128)(2,1)}, u32[]{:S(2)}) copy-start(bf16[384,256]{1,0:T(8,128)(2,1)} %param.17) | copy-start | bytes 589828
  134.9 16.1 %all-to-all-start.1 = ((f32[32,1,192]{2,1,0:T(1,128)}), f32[32,1,192]{2,1,0:T(1,128)S(1)}, u32[]{:S(2)}, u32[]{:S(2)}) async-start(f32[32,1,192]{2,1,0:T(1,128)} %broadcast_in_dim.147), calls=%async_computation.1 | async-start | bytes 65536 | tf_op jit(solution)/shard_map/all_to_all | solution.py:12
  151.3 4.7 collective-permute-start
  161.7 78.9 %all-to-all-start.2 = ((bf16[32,384,256]{2,1,0:T(8,128)(2,1)}), bf16[32,384,256]{2,1,0:T(8,128)(2,1)}, u32[]{:S(2)}, u32[]{:S(2)}) async-start(bf16[32,384,256]{2,1,0:T(8,128)(2,1)} %stack.11), calls=%async_computation.2 | async-start | bytes 12582912 | tf_op jit(solution)/shard_map/all_to_all | solution.py:47
  280.0 16.2 %all-to-all-start.3 = ((f32[32,1,192]{2,1,0:T(1,128)}), f32[32,1,192]{2,1,0:T(1,128)S(1)}, u32[]{:S(2)}, u32[]{:S(2)}) async-start(f32[32,1,192]{2,1,0:T(1,128)} %broadcast_in_dim.150), calls=%async_computation.3 | async-start | bytes 65536 | tf_op jit(solution)/shard_map/all_to_all | solution.py:12
  296.6 5.7 collective-permute-start.1
  307.9 79.1 %all-to-all-start.4 = ((bf16[32,384,256]{2,1,0:T(8,128)(2,1)}), bf16[32,384,256]{2,1,0:T(8,128)(2,1)}, u32[]{:S(2)}, u32[]{:S(2)}) async-start(bf16[32,384,256]{2,1,0:T(8,128)(2,1)} %stack.12), calls=%async_computation.4 | async-start | bytes 12582912 | tf_op jit(solution)/shard_map/all_to_all | solution.py:47
  426.5 16.0 %all-to-all-start.5 = ((f32[32,1,192]{2,1,0:T(1,128)}), f32[32,1,192]{2,1,0:T(1,128)S(1)}, u32[]{:S(2)}, u32[]{:S(2)}) async-start(f32[32,1,192]{2,1,0:T(1,128)} %broadcast_in_dim.153), calls=%async_computation.5 | async-start | bytes 65536 | tf_op jit(solution)/shard_map/all_to_all | solution.py:12
  442.9 5.7 collective-permute-start.2
  454.3 78.9 %all-to-all-start.6 = ((bf16[32,384,256]{2,1,0:T(8,128)(2,1)}), bf16[32,384,256]{2,1,0:T(8,128)(2,1)}, u32[]{:S(2)}, u32[]{:S(2)}) async-start(bf16[32,384,256]{2,1,0:T(8,128)(2,1)} %stack.13), calls=%async_computation.6 | async-start | bytes 12582912 | tf_op jit(solution)/shard_map/all_to_all | solution.py:47
  572.6 16.2 %all-to-all-start.7 = ((f32[32,1,192]{2,1,0:T(1,128)}), f32[32,1,192]{2,1,0:T(1,128)S(1)}, u32[]{:S(2)}, u32[]{:S(2)}) async-start(f32[32,1,192]{2,1,0:T(1,128)} %broadcast_in_dim.156), calls=%async_computation.7 | async-start | bytes 65536 | tf_op jit(solution)/shard_map/all_to_all | solution.py:12
  589.2 5.7 collective-permute-start.3
  600.5 79.1 %all-to-all-start.8 = ((bf16[32,384,256]{2,1,0:T(8,128)(2,1)}), bf16[32,384,256]{2,1,0:T(8,128)(2,1)}, u32[]{:S(2)}, u32[]{:S(2)}) async-start(bf16[32,384,256]{2,1,0:T(8,128)(2,1)} %stack.14), calls=%async_computation.8 | async-start | bytes 12582912 | tf_op jit(solution)/shard_map/all_to_all | solution.py:47
  719.1 16.0 %all-to-all-start.9 = ((f32[32,1,192]{2,1,0:T(1,128)}), f32[32,1,192]{2,1,0:T(1,128)S(1)}, u32[]{:S(2)}, u32[]{:S(2)}) async-start(f32[32,1,192]{2,1,0:T(1,128)} %broadcast_in_dim.160), calls=%async_computation.9 | async-start | bytes 65536 | tf_op jit(solution)/shard_map/all_to_all | solution.py:12
  735.4 0.6 copy-start.2
  736.0 0.7 copy-start.1
